TPU v7x, 32 devices: a whole 2x2x4 slice. The times are simulated.
32 devices in a mesh: width: 4 (over y, core), hidden: 8 (over z, x).
Axes of the slice: x: 2, y: 2, z: 4, core: 2. Of those that a mesh axis runs over, the one named last changes fastest.
Arguments:
- tokens: bfloat16 [1152, 5120], P(None, 'width'), may hold values from -6 to 6
- cotangent: bfloat16 [1152, 5120], P(None, 'width'), may hold values from -6 to 6
- w_up: bfloat16 [5120, 13824], P('width', 'hidden'), may hold values from -0.078125 to 0.078125
- bias_up: float32 [13824], P('hidden'), may hold values from -3 to 3
- w_down: bfloat16 [13824, 5120], P('hidden', 'width'), may hold values from -0.0546875 to 0.0546875
- mod_table: float32 [32, 3, 5120], P(None, None, 'width'), may hold values from -3 to 3
- seg_ids: int32 [1152], replicated, may hold values from 0 to 15, never falling along the last dimension, each value on 1 to 144 neighbouring positions
- step_ids: int32 [16], replicated, may hold values from 0 to 31
Outputs:
- grad_x: bfloat16 [1152, 5120], P(None, 'width')
- grad_up: float32 [5120, 13824], P('width', 'hidden')
- grad_down: float32 [13824, 5120], P('hidden', 'width')
- grad_bias: float32 [13824], P('hidden')
- grad_table: float32 [32, 3, 5120], P(None, None, 'width')
Inputs may be any that keep to these rules, and one draw needn't show every extreme that they name: `seg_ids`: request numbers never fall along the tokens and every request holds at least one token.
All inputs are finite; a program needn't handle non-finite values.
Results may differ from a plain program's by a relative error of at most 0.0063.
Values may be sent and summed in bfloat16 or wider, within the bound.
No kernel may reach another device: no remote copies, remote signals or barrier semaphores. Data moves between devices by JAX's collectives and lax.ppermute only.
A program may use at most 128 MiB of HBM per device.

v0:
```python
import jax
import jax.numpy as jnp
from jax import lax
from jax.sharding import PartitionSpec as P

D = 5120


def gelu_tanh(value):
    return jax.nn.gelu(value, approximate=True)


def norm_back(d_norm, x_hat, mod_gain, inv_std, cotangent):
    d_hat = d_norm * mod_gain
    feature_sums = lax.psum((jnp.sum(d_hat, 1), jnp.sum(d_hat * x_hat, 1)), "width")
    mean_one = feature_sums[0] / D
    mean_two = feature_sums[1] / D
    grad_rows = cotangent.astype(jnp.float32) + inv_std[:, None] * (
        d_hat - mean_one[:, None] - x_hat * mean_two[:, None]
    )
    return grad_rows.astype(jnp.bfloat16)


def per_device(tokens, cotangent, w_up, bias_up, w_down, mod_table, seg_ids, step_ids):
    highest = lax.Precision.HIGHEST
    req_count = step_ids.shape[0]
    table_rows = mod_table.shape[0]
    req_of = (seg_ids[:, None] == jnp.arange(req_count)[None, :]).astype(jnp.float32)
    step_of = (step_ids[:, None] == jnp.arange(table_rows)[None, :]).astype(jnp.float32)
    req_mod = jnp.einsum("rk,kcd->rcd", step_of, mod_table, precision=highest)
    shift_tok = jnp.dot(req_of, req_mod[:, 0], precision=highest)
    scale_tok = jnp.dot(req_of, req_mod[:, 1], precision=highest)
    gate_tok = jnp.dot(req_of, req_mod[:, 2], precision=highest)
    x_full = tokens.astype(jnp.float32)
    moment_one, moment_two = lax.psum((jnp.sum(x_full, 1), jnp.sum(x_full * x_full, 1)), "width")
    tok_mean = moment_one / D
    tok_var = moment_two / D - tok_mean * tok_mean
    inv_std = lax.rsqrt(tok_var + 1e-06)
    x_hat = (x_full - tok_mean[:, None]) * inv_std[:, None]
    mod_gain = 1.0 + scale_tok
    normed = (x_hat * mod_gain + shift_tok).astype(jnp.bfloat16)
    up_part = jnp.dot(normed, w_up, preferred_element_type=jnp.float32)
    pre_share = lax.psum_scatter(up_part, "width", scatter_dimension=0, tiled=True) + bias_up
    act_share = gelu_tanh(pre_share).astype(jnp.bfloat16)
    hidden_act = lax.all_gather(act_share, "width", axis=0, tiled=True)
    y_part = jnp.dot(hidden_act, w_down, preferred_element_type=jnp.float32)
    gate_part = jnp.dot(req_of.T, cotangent.astype(jnp.float32) * y_part, precision=highest)
    d_out = (cotangent.astype(jnp.float32) * gate_tok).astype(jnp.bfloat16)
    down_part = jnp.dot(d_out, w_down.T, preferred_element_type=jnp.float32)
    act_grad = lax.psum_scatter(down_part, "width", scatter_dimension=0, tiled=True)
    _, pull = jax.vjp(gelu_tanh, pre_share)
    pre_grad = pull(act_grad)[0]
    grad_bias = lax.psum(jnp.sum(pre_grad, 0), "width")
    d_pre_b = lax.all_gather(pre_grad.astype(jnp.bfloat16), "width", axis=0, tiled=True)
    grad_down = jnp.dot(hidden_act.T, d_out, preferred_element_type=jnp.float32)
    grad_up = jnp.dot(normed.T, d_pre_b, preferred_element_type=jnp.float32)
    d_part = jnp.dot(d_pre_b, w_up.T, preferred_element_type=jnp.float32)
    shift_part = jnp.dot(req_of.T, d_part, precision=highest)
    scale_part = jnp.dot(req_of.T, d_part * x_hat, precision=highest)
    req_grads = lax.psum(jnp.stack([shift_part, scale_part, gate_part], 1), "hidden")
    grad_table = jnp.einsum("rk,rcd->kcd", step_of, req_grads, precision=highest)
    d_norm = lax.psum(d_part, "hidden")
    grad_x = norm_back(d_norm, x_hat, mod_gain, inv_std, cotangent)
    return (grad_x, grad_up, grad_down, grad_bias, grad_table)


def solution(mesh):
    placed = (
        P(None, "width"),
        P(None, "width"),
        P("width", "hidden"),
        P("hidden"),
        P("hidden", "width"),
        P(None, None, "width"),
        P(),
        P(),
    )
    return jax.shard_map(
        per_device,
        mesh=mesh,
        in_specs=placed,
        out_specs=(
            P(None, "width"),
            P("width", "hidden"),
            P("hidden", "width"),
            P("hidden"),
            P(None, None, "width"),
        ),
        check_vma=False,
    )
```

profile of v0, /device:TPU:0, one launch (start us, length us, event | category | flops | bytes accessed | tf_op | source)
XLA Modules:
  0.0 515.7 jit_solution(15026594114937513184)
XLA Ops:
  7.2 0.0 copy-start
  7.2 0.0 copy-start.2
  7.2 0.0 copy-start.9
  7.2 0.0 reduce-scatter.5.cloned.1.call-start
  7.3 2.9 fusion.3
  10.1 12.7 %all-reduce.2 = (f32[1152]{0:T(1024)S(1)}, f32[1152]{0:T(1024)S(1)}) all-reduce(f32[1152]{0:T(1024)S(1)} %get-tuple-element.8, f32[1152]{0:T(1024)S(1)} %get-tuple-element.7), channel_id=1, replica_groups=mesh['width'=4,'hidden'=8] {'width'}, use_global_device_ids=true, to_apply=%region_3.0 | all-reduce | flops 2304 | bytes 18432 | tf_op jit(solution)/shard_map/psum | solution.py:35
  22.9 0.0 copy-done
  22.9 1.0 fusion.34
  23.9 0.0 copy-start.8
  23.9 0.0 slice-start
  23.9 3.4 convolution_add_fusion.1
  27.2 0.0 copy-start.3
  27.3 0.0 copy-done.8
  27.3 2.5 copy-done.3
  29.8 0.0 copy-done.2
  29.8 0.0 copy-done.9
  29.8 0.0 slice-start.1
  29.8 3.7 fusion.1
  33.5 0.0 copy-start.5
  33.6 1.6 copy-done.5
  35.1 0.0 slice-done
  35.1 0.0 slice-done.1
  35.2 7.7 %fusion.42 = f32[1152,1728]{1,0:T(8,128)} fusion(bf16[1152,1280]{1,0:T(8,128)(2,1)S(1)} %fusion.1, bf16[1280,1728]{0,1:T(8,128)(2,1)S(1)} %bitcast.36), kind=kOutput, calls=%fused_computation.59 | convolution fusion | flops 5096079360 | bytes 15335424 | tf_op jit(solution)/shard_map/dot_general | solution.py:42
  42.9 0.0 reduce-scatter.5.cloned.1.call-update
  42.9 0.0 reduce-scatter.3.cloned.1.call-start
  43.0 4.5 fusion
  47.4 0.0 copy-start.6
  47.5 1.7 copy-done.6
  49.1 10.2 %fusion.41 = f32[1152,1728]{1,0:T(8,128)} fusion(bf16[1152,1280]{1,0:T(8,128)(2,1)S(1)} %fusion, bf16[1728,1280]{1,0:T(8,128)(2,1)} %param.12), kind=kOutput, calls=%fused_computation.58 | convolution fusion | flops 5096079360 | bytes 15335424 | tf_op jit(solution)/shard_map/dot_general | solution.py:49
  59.4 0.0 reduce-scatter.3.cloned.1.call-update
  59.4 0.2 all-gather.3.cloned.1.call-start
  59.6 54.3 %reduce-scatter.5.cloned.1.call-done = f32[288,1728]{1,0:T(8,128)} async-done(((f32[1152,1728]{1,0:T(8,128)}), f32[288,1728]{1,0:T(8,128)}) %reduce-scatter.5.cloned.1.call-update) | async-done | bytes 1990672 | tf_op jit(solution)/shard_map/reduce_scatter | solution.py:43
  113.9 73.9 %reduce-scatter.3.cloned.1.call-done = f32[288,1728]{1,0:T(8,128)} async-done(((f32[1152,1728]{1,0:T(8,128)}), f32[288,1728]{1,0:T(8,128)}) %reduce-scatter.3.cloned.1.call-update) | async-done | bytes 1990672 | tf_op jit(solution)/shard_map/reduce_scatter | solution.py:50
  187.8 0.0 copy-done.11
  187.8 5.1 fusion.39
  192.9 0.0 all-gather.3.cloned.1.call-update
  193.0 0.0 all-gather.5.cloned.1.call-start
  193.0 0.5 all-gather.5.cloned.1.call-update
  193.5 0.0 all-reduce.5.cloned.1.call-start
  193.6 33.6 %all-gather.3.cloned.1.call-done = bf16[1152,1728]{1,0:T(8,128)(2,1)} async-done(((bf16[288,1728]{1,0:T(8,128)(2,1)}), bf16[1152,1728]{1,0:T(8,128)(2,1)}) %all-gather.3.cloned.1.call-update) | async-done | bytes 3981328 | tf_op jit(solution)/shard_map/all_gather | solution.py:54
  227.2 8.6 %fusion.43 = f32[1152,1280]{1,0:T(8,128)S(1)} fusion(bf16[1152,1728]{1,0:T(8,128)(2,1)} %all-gather.3.cloned.1.call-done, bf16[1280,1728]{0,1:T(8,128)(2,1)} %param.10), kind=kOutput, calls=%fused_computation.60 | convolution fusion | flops 5096079360 | bytes 14303232 | tf_op jit(solution)/shard_map/dot_general | solution.py:57
  235.8 0.0 copy-start.4
  235.8 2.1 convolution_bitcast_fusion.1
  237.9 0.8 copy-done.4
  238.7 2.8 fusion.16
  241.5 21.8 %all-gather.5.cloned.1.call-done = bf16[1152,1728]{1,0:T(8,128)(2,1)} async-done(((bf16[288,1728]{1,0:T(8,128)(2,1)}), bf16[1152,1728]{1,0:T(8,128)(2,1)}) %all-gather.5.cloned.1.call-update) | async-done | bytes 3981328 | tf_op jit(solution)/shard_map/all_gather | solution.py:45
  263.3 9.0 %convolution_multiply_fusion = f32[1152,1280]{1,0:T(8,128)S(1)} fusion(bf16[1152,1728]{1,0:T(8,128)(2,1)} %all-gather.5.cloned.1.call-done, bf16[1728,1280]{1,0:T(8,128)(2,1)} %param.12, bf16[1152,1280]{1,0:T(8,128)(2,1)} %param.9), kind=kOutput, calls=%fused_computation | convolution fusion | flops 5099028480 | bytes 17252352 | tf_op jit(solution)/shard_map/dot_general | solution.py:46
  272.4 2.1 convolution_bitcast_fusion
  274.5 0.7 pad_maximum_fusion
  275.2 0.0 all-reduce.5.cloned.1.call-update
  275.3 0.0 copy-start.7
  275.3 0.0 copy-start.13
  275.3 11.3 %fusion.44 = f32[1280,1728]{0,1:T(8,128)} fusion(bf16[1152,1280]{1,0:T(8,128)(2,1)} %copy-done.5, bf16[1152,1728]{1,0:T(8,128)(2,1)} %all-gather.3.cloned.1.call-done), kind=kOutput, calls=%fused_computation.61 | convolution fusion | flops 5096079360 | bytes 15777792 | tf_op jit(solution)/shard_map/dot_general | solution.py:56
  286.5 0.0 copy-done.7
  286.5 0.0 copy-done.13
  286.5 8.6 %fusion.45 = f32[1728,1280]{1,0:T(8,128)} fusion(bf16[1152,1728]{1,0:T(8,128)(2,1)S(1)} %copy-done.13, bf16[1152,1280]{1,0:T(8,128)(2,1)S(1)} %copy-done.7), kind=kOutput, calls=%fused_computation.62 | convolution fusion | flops 5096079360 | bytes 15777792 | tf_op jit(solution)/shard_map/dot_general | solution.py:55
  295.1 187.8 %all-reduce.5.cloned.1.call-done = (f32[1152,1280]{1,0:T(8,128)}, f32[16,3,1280]{2,0,1:T(8,128)}) async-done(((f32[1152,1280]{1,0:T(8,128)}, f32[16,3,1280]{2,0,1:T(8,128)}), (f32[1152,1280]{1,0:T(8,128)}, f32[16,3,1280]{2,0,1:T(8,128)})) %all-reduce.5.cloned.1.call-update) | async-done | bytes 6144016 | tf_op jit(solution)/shard_map/psum | solution.py:62
  482.9 8.0 %fusion.38 = (f32[1152]{0:T(1024)S(1)}, f32[1152]{0:T(1024)S(1)}, f32[1152,1280]{1,0:T(8,128)}) fusion(f32[1152]{0:T(1024)S(1)} %get-tuple-element.21, f32[1152]{0:T(1024)S(1)} %get-tuple-element.20, bf16[1152,1280]{1,0:T(8,128)(2,1)S(1)} %copy-done.2, f32[1152,1280]{1,0:T(8,128)} %get-tuple-element.9, f32[1152,1280]{1,0:T(8,128)} %copy-done.3), kind=kLoop, calls=%fused_computation.56 | loop fusion | flops 10319616 | bytes 20662272 | tf_op jit(solution)/shard_map/reduce_sum | solution.py:15
  490.8 0.0 copy-done.10
  490.8 0.0 copy-done.12
  490.8 1.3 fusion.32
  492.1 11.2 %all-reduce.1 = (f32[1152]{0:T(1024)S(1)}, f32[1152]{0:T(1024)S(1)}, f32[1728]{0:T(1024)}) all-reduce(f32[1152]{0:T(1024)S(1)} %get-tuple-element.6, f32[1152]{0:T(1024)S(1)} %get-tuple-element.5, f32[1728]{0:T(1024)S(1)} %get-tuple-element.16), channel_id=1, replica_groups=mesh['width'=4,'hidden'=8] {'width'}, use_global_device_ids=true, to_apply=%region_10.0 | all-reduce | flops 4032 | bytes 32256 | tf_op jit(solution)/shard_map/psum | solution.py:15
  503.3 5.9 %fusion.2 = bf16[1152,1280]{1,0:T(8,128)(2,1)} fusion(bf16[1152,1280]{1,0:T(8,128)(2,1)} %param.9, bf16[1152,1280]{1,0:T(8,128)(2,1)S(1)} %copy-done.2, f32[1152,1280]{1,0:T(8,128)} %get-tuple-element.18, f32[1152]{0:T(1024)S(1)} %get-tuple-element.22, f32[1152]{0:T(1024)S(1)} %get-tuple-element.23, f32[1152]{0:T(1024)S(1)} %get-tuple-element.20, ...), kind=kLoop, calls=%fused_computation.10 | loop fusion | flops 14745600 | bytes 14764032 | tf_op jit(solution)/shard_map/convert_element_type | solution.py:21
  509.1 0.0 copy-done.1
  (7 shorter events, 0.0 us)
Async XLA Ops:
  7.2 15.7 %copy-start = (f32[32,3,1280]{2,0,1:T(8,128)S(1)}, f32[32,3,1280]{2,0,1:T(8,128)}, u32[]{:S(2)}) copy-start(f32[32,3,1280]{2,0,1:T(8,128)} %param.13) | copy-start | bytes 1474564
  7.2 22.6 %copy-start.2 = (bf16[1152,1280]{1,0:T(8,128)(2,1)S(1)}, bf16[1152,1280]{1,0:T(8,128)(2,1)}, u32[]{:S(2)}) copy-start(bf16[1152,1280]{1,0:T(8,128)(2,1)} %param.8) | copy-start | bytes 8847364
  7.2 22.6 %copy-start.9 = (s32[1152]{0:T(1024)S(1)}, s32[1152]{0:T(1024)}, u32[]{:S(2)}) copy-start(s32[1152]{0:T(1024)} %param.14) | copy-start | bytes 13828
  7.2 106.7 %reduce-scatter.5.cloned.1.call-start = ((), (), s32[]{:S(2)}) async-start(), calls=%async_computation.3 | async-start | bytes 10321920 | tf_op jit(solution)/shard_map/reduce_scatter | solution.py:43
  23.9 3.4 copy-start.8
  23.9 11.3 %slice-start = ((s8[4423680]{0:T(1024)(128)(4,1)}), s8[4194304]{0:T(1024)(128)(4,1)S(1)}, s32[]{:S(2)}) async-start(s8[4423680]{0:T(1024)(128)(4,1)} %bitcast.35), calls=%async_computation.7 | async-start | bytes 8388608
  27.2 2.5 copy-start.3
  29.8 5.4 %slice-start.1 = ((s8[4423680]{0:T(1024)(128)(4,1)}), s8[229376]{0:T(1024)(128)(4,1)S(1)}, s32[]{:S(2)}) async-start(s8[4423680]{0:T(1024)(128)(4,1)} %bitcast.35), calls=%async_computation.8 | async-start | bytes 458752
  33.5 1.6 copy-start.5
  42.9 144.9 %reduce-scatter.3.cloned.1.call-start = ((), (), s32[]{:S(2)}) async-start(), calls=%async_computation.2 | async-start | bytes 10321920 | tf_op jit(solution)/shard_map/reduce_scatter | solution.py:50
  47.4 1.7 copy-start.6
  59.4 128.5 %copy-start.11 = (f32[1728]{0:T(1024)S(1)}, f32[1728]{0:T(1024)}, u32[]{:S(2)}) copy-start(f32[1728]{0:T(1024)} %param.11) | copy-start | bytes 20740
  59.4 167.8 %all-gather.3.cloned.1.call-start = ((), (), s32[]{:S(2)}) async-start(), calls=%async_computation.4 | async-start | bytes 5160960 | tf_op jit(solution)/shard_map/all_gather | solution.py:54
  193.0 70.4 %all-gather.5.cloned.1.call-start = ((), (), s32[]{:S(2)}) async-start(), calls=%async_computation.5 | async-start | bytes 5160960 | tf_op jit(solution)/shard_map/all_gather | solution.py:45
  193.5 289.3 %all-reduce.5.cloned.1.call-start = ((), (), s32[]{:S(2)}) async-start(), calls=%async_computation.6 | async-start | bytes 12288000 | tf_op jit(solution)/shard_map/psum | solution.py:62
  235.8 2.9 copy-start.4
  275.3 11.3 %copy-start.7 = (bf16[1152,1280]{1,0:T(8,128)(2,1)S(1)}, bf16[1152,1280]{1,0:T(8,128)(2,1)}, u32[]{:S(2)}) copy-start(bf16[1152,1280]{1,0:T(8,128)(2,1)} %copy-done.6) | copy-start | bytes 8847364
  275.3 11.3 %copy-start.13 = (bf16[1152,1728]{1,0:T(8,128)(2,1)S(1)}, bf16[1152,1728]{1,0:T(8,128)(2,1)}, u32[]{:S(2)}) copy-start(bf16[1152,1728]{1,0:T(8,128)(2,1)} %all-gather.5.cloned.1.call-done) | copy-start | bytes 11943940
  482.9 8.0 %copy-start.10 = (f32[16,3,1280]{2,0,1:T(8,128)S(1)}, f32[16,3,1280]{2,0,1:T(8,128)}, u32[]{:S(2)}) copy-start(f32[16,3,1280]{2,0,1:T(8,128)} %get-tuple-element.10) | copy-start | bytes 737284
  482.9 8.0 %copy-start.12 = (s32[16]{0:T(128)S(1)}, s32[16]{0:T(128)}, u32[]{:S(2)}) copy-start(s32[16]{0:T(128)} %param.15) | copy-start | bytes 196
  503.3 5.9 %copy-start.1 = (f32[32,3,1280]{2,0,1:T(8,128)S(1)}, f32[32,3,1280]{2,0,1:T(8,128)}, u32[]{:S(2)}) copy-start(f32[32,3,1280]{2,0,1:T(8,128)} %param.13) | copy-start | bytes 1474564
Sparse Core Ops, SparseCore 0:
  43.0 70.8 reduce-scatter.4
  117.2 70.6 reduce-scatter.2
  193.1 34.0 all-gather.2
  229.2 34.0 all-gather.4
  275.4 207.4 all-reduce.4
where the time goes:
time: 516 us
  waiting for transfers between devices  372 us (72%)
  matrix products  76.3 us (15%)
  blocking collectives  23.9 us (5%)
  other arithmetic  22.6 us (4%)
  between operations  13.9 us (3%)
  local copies, waits for them, and re-layouts  6.61 us (1%)
    psum x1, waiting for transfers between devices, per_device(): d_norm = lax.psum(d_part, 'hidden')  188 us
    reduce_scatter x1, waiting for transfers between devices, per_device(): lax.psum_scatter(down_part, 'width', scatter_dimension=0, tiled=True)  73.9 us
    reduce_scatter x1, waiting for transfers between devices, per_device(): lax.psum_scatter(up_part, 'width', scatter_dimension=0, tiled=True)  54.3 us
    all_gather x1, waiting for transfers between devices, per_device(): lax.all_gather(pre_grad.astype(jnp.bfloat16), 'width', axis=0, tiled=True)  33.6 us
    all_gather x1, waiting for transfers between devices, per_device(): hidden_act = lax.all_gather(act_share, 'width', axis=0, tiled=True)  21.8 us
    psum x1, blocking collectives, per_device(): lax.psum((jnp.sum(x_full, 1), jnp.sum(x_full * x_full, 1)), 'width')  12.7 us
    dot_general x1, matrix products, per_device(): grad_up = jnp.dot(normed.T, d_pre_b, preferred_element_type=jnp.float32)  11.3 us
    psum x1, blocking collectives, norm_back(): lax.psum((jnp.sum(d_hat, 1), jnp.sum(d_hat * x_hat, 1)), 'width')  11.2 us
  transfers between devices with their start and end apart: 5, of which 5 were waited for; matrix products, arithmetic and copies ran while one was open for 9% of the time, Pallas kernels for 0%

commit v1 on v0

v1 whole, which is shorter than its diff:
```python
import functools

import jax
import jax.numpy as jnp
from jax import lax
from jax.experimental import pallas as pl
from jax.experimental.pallas import tpu as pltpu
from jax.sharding import PartitionSpec as P


SPLIT = (3, 3, 2, 1)
TILE = 64
BLOCK_N = 256
BLOCK_D = 256
PLAN = tuple(
    (word.rstrip("0123456789"), int(word[-1]))
    for line in (
        "mid0 part0 mid1 ra0",
        "part1 rb0 mid2 mid3",
        "part2 ra1 na0 part3",
        "nb0 rb1 ra2 ra3",
        "gate0 ga0 rb2 rb3",
        "na1 down0 gb0 na2",
        "nb1 na3 nb2 nb3",
        "ga1 up0 ga2 ga3",
        "gb1 gb2 gb3",
        "fin0 fin1 fin2 fin3",
    )
    for word in line.split()
)


def f32(value):
    return value.astype(jnp.float32)


def bf16(value):
    return value.astype(jnp.bfloat16)


def swap(value, axis, mask, size):
    return lax.ppermute(value, axis, [(i, i ^ mask) for i in range(size)])


def sum_all(value, axis, size):
    terms = [value] + [swap(value, axis, mask, size) for mask in range(1, size)]
    while len(terms) > 1:
        terms = [terms[i] + terms[i + 1] for i in range(0, len(terms), 2)]
    return terms[0]


def sum_pairs(value, axis, mask, size):
    while mask < size:
        value = value + swap(value, axis, mask, size)
        mask *= 2
    return value


def round_off(value):
    return lax.reduce_precision(value, 8, 7)


def three_parts(value):
    first = round_off(value)
    second = round_off(value - first)
    third = value - first - second
    return bf16(jnp.concatenate([first, second, third], 0))


def mm(a, b, dims):
    return lax.dot_general(a, b, (dims, ((), ())), preferred_element_type=jnp.float32)


def tie(values, other):
    values = list(values)
    *values, _ = lax.optimization_barrier((*values, other))
    return values


def look(seg, table):
    wide = table.shape[0]
    reqs = wide // 3
    lanes = lax.broadcasted_iota(jnp.int32, (seg.shape[0], wide), 1)
    hot = (lanes == seg) | (lanes == seg + reqs) | (lanes == seg + 2 * reqs)
    return mm(jnp.where(hot, 1.0, 0.0).astype(jnp.bfloat16), table, ((1,), (0,)))


def call(kernel, grid, prefetch, in_specs, out_specs, out_shape, cost, aliases=None):
    return pl.pallas_call(
        kernel,
        out_shape=out_shape,
        grid_spec=pltpu.PrefetchScalarGridSpec(
            num_scalar_prefetch=prefetch, grid=grid, in_specs=in_specs, out_specs=out_specs
        ),
        input_output_aliases=aliases or {},
        cost_estimate=pl.CostEstimate(flops=cost[0], bytes_accessed=cost[1], transcendentals=0),
    )


def shape(dims, dtype=jnp.bfloat16):
    return jax.ShapeDtypeStruct(dims, dtype)


def project_pieces(pieces, lhs, w, outs):
    total = bf16(mm(lhs[...], w[...], ((1,), (1,))))
    for (start, size), out in zip(pieces, outs):
        out[...] = total[start:start + size]


def project_d_kernel(pieces, order, dep, cot, seg, gate, w, lhs, cot_out, hot_out, *outs):
    @pl.when(pl.program_id(0) == 0)
    def _():
        def step(t, carry):
            src = pl.ds(pl.multiple_of(order[t] * TILE, TILE), TILE)
            dst = pl.ds(pl.multiple_of(t * TILE, TILE), TILE)
            ids = seg[src, :]
            value = cot[src, :]
            lhs[dst, :] = bf16(f32(value) * look(ids, gate[...]))
            cot_out[dst, :] = value
            lanes = lax.broadcasted_iota(jnp.int32, (TILE, hot_out.shape[1]), 1)
            hot_out[dst, :] = jnp.where(lanes == ids, 1.0, 0.0).astype(jnp.bfloat16)
            return carry

        lax.fori_loop(0, lhs.shape[0] // TILE, step, 0)

    project_pieces(pieces, lhs, w, outs)


def project_u_kernel(pieces, order, dep, tok, seg, st, shift, scale, w, lhs, *outs):
    @pl.when(pl.program_id(0) == 0)
    def _():
        def step(t, carry):
            src = pl.ds(pl.multiple_of(order[t] * TILE, TILE), TILE)
            dst = pl.ds(pl.multiple_of(t * TILE, TILE), TILE)
            ids = seg[src, :]
            x_hat = (f32(tok[src, :]) - st[src, 0:1]) * st[src, 1:2]
            lhs[dst, :] = bf16(x_hat * (1.0 + look(ids, scale[...])) + look(ids, shift[...]))
            return carry

        lax.fori_loop(0, lhs.shape[0] // TILE, step, 0)

    project_pieces(pieces, lhs, w, outs)


def mid_kernel(dep, ds, dr, us, ur, bias, out, total):
    value = f32(us[...]) + f32(ur[...]) + bias[...]
    root = 0.7978845608028654
    square = value * value
    bent = jnp.tanh(root * (value + 0.044715 * (value * square)))
    half = 0.5 * (1.0 + bent)
    slope = half + 0.5 * value * (1.0 - bent * bent) * (root * (1.0 + 0.134145 * square))
    d_pre = (f32(ds[...]) + f32(dr[...])) * slope
    out[0] = bf16(value * half)
    out[1] = bf16(d_pre)

    @pl.when(pl.program_id(0) == 0)
    def _():
        total[...] = jnp.zeros_like(total)

    total[...] += jnp.sum(d_pre, 0, keepdims=True)


def part_kernel(first, flags, dep, own, oth, w, *refs):
    send, keep, act_all, grad_all = refs[0 if first else 2:]
    half = own.shape[1]

    @pl.when(pl.program_id(0) == 0)
    def _():
        for side, ref in enumerate((own, oth)):
            act_all[side * half:(side + 1) * half, :] = ref[0]
            grad_all[side * half:(side + 1) * half, :] = ref[1]

    total = bf16(mm(grad_all[...], w[...], ((1,), (0,))))

    @pl.when(flags[0] == 1)
    def _():
        send[...] = total[half:]
        keep[...] = total[:half]

    @pl.when(flags[0] == 0)
    def _():
        send[...] = total[:half]
        keep[...] = total[half:]


def norm_a_kernel(q, dep, keep, got, tok, st, seg, scale, sums, table):
    d = keep[...] + f32(got[...])
    x_hat = (f32(tok[...]) - st[:, 0:1]) * st[:, 1:2]
    d_hat = d * (1.0 + look(seg[...], scale[...]))
    one = jnp.sum(d_hat, 1, keepdims=True)
    two = jnp.sum(d_hat * x_hat, 1, keepdims=True)
    lane = lax.broadcasted_iota(jnp.int32, sums.shape, 1)
    sums[...] = jnp.where(lane == 0, one, jnp.where(lane == 1, two, 0.0))
    reqs = table.shape[1]
    ids = lax.broadcasted_iota(jnp.int32, (d.shape[0], reqs), 1)
    hot = jnp.where(ids == seg[...], 1.0, 0.0).astype(jnp.bfloat16)
    for c, value in enumerate((d, d * x_hat)):
        top = bf16(value)
        low = bf16(value - f32(top))
        table[c] = mm(hot, top, ((0,), (0,))) + mm(hot, low, ((0,), (0,)))


def norm_b_kernel(dim, q, dep, keep, got, tok, cot, st, seg, scale, sums, out):
    d = keep[...] + f32(got[...])
    inv = st[:, 1:2]
    x_hat = (f32(tok[...]) - st[:, 0:1]) * inv
    d_hat = d * (1.0 + look(seg[...], scale[...]))
    means = sums[...] * (1.0 / dim)
    out[...] = bf16(f32(cot[...]) + inv * (d_hat - means[:, 0:1] - x_hat * means[:, 1:2]))


def make_body(nw, nh):
    def body(tokens, cotangent, w_up, bias_up, w_down, mod_table, seg_ids, step_ids):
        count, dw = tokens.shape
        fh = w_up.shape[1]
        dim = dw * nw
        reqs, rows_of = step_ids.shape[0], mod_table.shape[0]
        highest = lax.Precision.HIGHEST
        core = lax.axis_index("width") % 2
        me = lax.axis_index("hidden")
        step_of = f32(step_ids[:, None] == jnp.arange(rows_of)[None, :])
        req_mod = jnp.einsum("rk,kcd->crd", step_of, mod_table, precision=highest)
        shift3, scale3, gate3 = [three_parts(req_mod[c]) for c in range(3)]
        seg = seg_ids[:, None]

        x_full = f32(tokens)
        moments = jnp.stack([jnp.sum(x_full, 1), jnp.sum(x_full * x_full, 1)])
        sums = sum_all(moments, "width", nw)
        mean = sums[0] / dim
        inv_std = lax.rsqrt(sums[1] / dim - mean * mean + 1e-06)
        stats = jnp.stack([mean, inv_std], 1)

        unit = count // sum(SPLIT)
        chunks, start = [], 0
        for s in SPLIT:
            chunks.append((start, s * unit))
            start += s * unit
        core_arr = core.astype(jnp.int32)[None]
        near, flip = [], []
        for at, n in chunks:
            tiles = n // TILE
            near += [at // TILE + t for t in range(tiles)]
            flip += [at // TILE + (t + tiles // 2) % tiles for t in range(tiles)]
        order = jnp.where(core == 0, jnp.array(near, jnp.int32), jnp.array(flip, jnp.int32))

        def plain(rows, cols):
            return pl.BlockSpec((rows, cols), lambda j, *_: (0, 0))

        def rows_spec(cols):
            return pl.BlockSpec((TILE, cols), lambda j, *_: (j, 0))

        pieces = [(at + side * (n // 2), n // 2) for at, n in chunks for side in range(2)]
        steps = pl.cdiv(fh, BLOCK_N)

        anywhere = pl.BlockSpec(memory_space=pl.ANY)

        def project(kernel, ins, specs, w, extra):
            return call(
                functools.partial(kernel, pieces), (steps,), 1,
                [anywhere] + specs + [pl.BlockSpec((BLOCK_N, dw), lambda j, *_: (j, 0))],
                [plain(*e.shape) for e in extra]
                + [pl.BlockSpec((size, BLOCK_N), lambda j, *_: (0, j)) for _, size in pieces],
                extra + [shape((size, fh)) for _, size in pieces],
                (count * fh * dw * 2, fh * dw * 2 + count * (fh + 3 * dw) * 2),
            )(order, *ins, w)

        pairs = [None] * (2 * len(chunks))

        def exchange(i, k, parts, dep):
            own, oth = parts[2 * i:2 * i + 2]
            own, got = tie((own, swap(oth, "width", 1, nw)), dep)
            value = bf16(f32(own) + f32(got))
            dep = value
            mask = 2
            while 2 * mask < nw:
                value = bf16(f32(value) + f32(swap(value, "width", mask, nw)))
                mask *= 2
            pairs[2 * i + k] = (value, swap(value, "width", mask, nw))
            return dep

        d_all, cot_all, hot_all, *d_parts = project(
            project_d_kernel, [moments, cotangent, seg, gate3],
            [plain(count, dw), plain(count, 1), plain(3 * reqs, dw)], w_down,
            [shape((count, dw)), shape((count, dw)), shape((count, 128))],
        )
        last_chunk = len(chunks) - 1
        dep = exchange(0, 0, d_parts, d_parts[0])
        dep = exchange(last_chunk, 0, d_parts, dep)
        w_up_t = w_up.T
        n_all, *u_parts = project(
            project_u_kernel, [dep, tokens, seg, stats, shift3, scale3],
            [plain(count, dw), plain(count, 1), plain(count, 2)] + [plain(3 * reqs, dw)] * 2, w_up_t,
            [shape((count, dw))],
        )
        dep = exchange(0, 1, u_parts, u_parts[0])
        for i in range(1, len(chunks)):
            if i < last_chunk:
                dep = exchange(i, 0, d_parts, dep)
            dep = exchange(i, 1, u_parts, dep)

        masks = []
        while 2 ** len(masks) < nh:
            masks.append(2 ** len(masks))
        bits = [(me // mask) % 2 for mask in masks]
        spot = 0
        for bit in bits:
            spot = spot * 2 + bit
        xbit = bits[0]
        flag = (xbit == core).astype(jnp.int32)[None]
        spot_arr = spot.astype(jnp.int32)[None]
        bias_row = bias_up[None]
        state = {"bias": 0.0, "table": 0.0, "buffers": [], "out": jnp.zeros((count, dw), jnp.bfloat16)}
        boths, gots, feats, grads = {}, {}, {}, {}

        def mid(i, dep):
            half = chunks[i][1] // 2
            both, total = call(
                mid_kernel, (half // TILE,), 0,
                [anywhere] + [rows_spec(fh)] * 4 + [plain(1, fh)],
                [pl.BlockSpec((2, TILE, fh), lambda j: (0, j, 0)), plain(1, fh)],
                [shape((2, half, fh)), shape((1, fh), jnp.float32)], (half * fh * 30, half * fh * 12),
            )(dep, *pairs[2 * i], *pairs[2 * i + 1], bias_row)
            state["bias"] = state["bias"] + total[0]
            boths[i] = (both, swap(both, "width", 1, nw))
            return total

        def part(i, dep):
            at, n = chunks[i]
            half = n // 2
            buffers = state["buffers"]
            cols = BLOCK_D if dw % BLOCK_D == 0 else dw
            whole = pl.BlockSpec((2, half, fh), lambda j, *_: (0, 0, 0))
            here = pl.BlockSpec((n, fh), lambda j, *_: (at // n, 0))
            send, keep, *buffers = call(
                functools.partial(part_kernel, not buffers), (dw // cols,), 1,
                [anywhere, whole, whole, pl.BlockSpec((fh, cols), lambda j, *_: (0, j))] + [anywhere] * len(buffers),
                [pl.BlockSpec((half, cols), lambda j, *_: (0, j))] * 2 + [here, here],
                [shape((half, dw)), shape((half, dw)), shape((count, fh)), shape((count, fh))],
                (n * fh * dw * 2, n * fh * 8 + fh * dw * 2 + n * dw * 2),
                {5: 2, 6: 3} if buffers else None,
            )(flag, dep, *boths[i], w_up_t, *buffers)
            state["buffers"] = buffers
            gots[i] = (keep, swap(send, "hidden", 1, nh))
            return keep

        def halve(i, dep, which):
            for k in which:
                keep, got = tie(gots[i], dep)
                value = (f32(keep) + f32(got)).reshape(2, -1, dw)
                send = bf16(lax.dynamic_index_in_dim(value, 1 - bits[k], 0, keepdims=False))
                dep = send
                got = swap(send, "hidden", masks[k], nh)
                gots[i] = (lax.dynamic_index_in_dim(value, bits[k], 0, keepdims=False), got)
            return dep

        def double(i, dep, which):
            for k in which:
                grad, got = tie(grads[i], dep)
                grad = jnp.where(bits[k] == 0, jnp.stack([grad, got]), jnp.stack([got, grad])).reshape(-1, dw)
                dep = grad
                grads[i] = (grad, swap(grad, "hidden", masks[k - 1], nh))
            return dep

        def places(i):
            at, n = chunks[i]
            rows = n // nh
            if rows % 16 == 0 and at % rows == 0:
                return rows, lambda v: v, lambda cols: pl.BlockSpec((rows, cols), lambda j, q: (at // rows + q[0], 0))
            return rows, lambda v: lax.dynamic_slice_in_dim(v, at + spot * rows, rows, 0), lambda cols: plain(rows, cols)

        def norm_a(i, dep):
            rows, mine, own_spec = places(i)
            sums_part, table_new = call(
                norm_a_kernel, (1,), 1,
                [anywhere, plain(rows, dw), plain(rows, dw), own_spec(dw), own_spec(2), own_spec(1), plain(3 * reqs, dw)],
                [plain(rows, 128), pl.BlockSpec((2, reqs, dw), lambda j, *_: (0, 0, 0))],
                [shape((rows, 128), jnp.float32), shape((2, reqs, dw), jnp.float32)],
                (rows * dw * 200, rows * dw * 16),
            )(spot_arr, dep, *gots[i], mine(tokens), mine(stats), mine(seg), scale3)
            state["table"] = state["table"] + table_new
            feats[i] = sum_all(sums_part, "width", nw)
            return sums_part

        def norm_b(i, dep):
            rows, mine, own_spec = places(i)
            grad = call(
                functools.partial(norm_b_kernel, dim), (1,), 1,
                [anywhere, plain(rows, dw), plain(rows, dw), own_spec(dw), own_spec(dw), own_spec(2), own_spec(1), plain(3 * reqs, dw), plain(rows, 128)],
                plain(rows, dw), shape((rows, dw)), (rows * dw * 200, rows * dw * 12),
            )(spot_arr, dep, *gots[i], mine(tokens), mine(cotangent), mine(stats), mine(seg), scale3, feats[i])
            grads[i] = (grad, swap(grad, "hidden", masks[-1], nh))
            return grad

        def finish(i, dep):
            at, n = chunks[i]
            grad, other = tie(grads[i], dep)
            out = lax.dynamic_update_slice(state["out"], grad, (at + xbit * (n // 2), 0))
            state["out"] = lax.dynamic_update_slice(out, other, (at + (1 - xbit) * (n // 2), 0))
            return grad

        def down(i, dep):
            act_all, = tie((state["buffers"][0],), dep)
            state["down"] = mm(act_all, d_all, ((0,), (0,)))
            return state["down"]

        def up(i, dep):
            grad_all, = tie((state["buffers"][1],), dep)
            state["up"] = mm(grad_all, n_all, ((0,), (0,)))
            return state["up"]

        def gate(i, dep):
            act_all, = tie((state["buffers"][0],), dep)
            y_cot = bf16(f32(cot_all) * mm(act_all, w_down, ((1,), (0,))))
            state["gate"] = mm(hot_all, y_cot, ((0,), (0,)))[:reqs]
            return state["gate"]

        count_masks = len(masks)
        stages = {
            "mid": mid, "part": part, "na": norm_a, "nb": norm_b, "fin": finish, "down": down, "up": up, "gate": gate,
            "ra": lambda i, dep: halve(i, dep, range(1, 2)),
            "rb": lambda i, dep: halve(i, dep, range(2, count_masks)),
            "ga": lambda i, dep: double(i, dep, range(count_masks - 1, 1, -1)),
            "gb": lambda i, dep: double(i, dep, range(1, 0, -1)),
        }
        for stage, i in PLAN:
            dep = stages[stage](i, dep)

        table = sum_pairs(jnp.concatenate([state["table"], state["gate"][None]], 0), "hidden", 1, nh)
        grad_table = jnp.einsum("rk,crd->kcd", step_of, table, precision=highest)
        grad_bias = state["bias"] + swap(state["bias"], "width", 1, nw)
        return state["out"], state["up"].T, state["down"], grad_bias, grad_table

    return body


def solution(mesh):
    body = make_body(mesh.shape["width"], mesh.shape["hidden"])

    return jax.shard_map(
        body,
        mesh=mesh,
        in_specs=(
            P(None, "width"),
            P(None, "width"),
            P("width", "hidden"),
            P("hidden"),
            P("hidden", "width"),
            P(None, None, "width"),
            P(),
            P(),
        ),
        out_specs=(
            P(None, "width"),
            P("width", "hidden"),
            P("hidden", "width"),
            P("hidden"),
            P(None, None, "width"),
        ),
        check_vma=False,
    )
```

time: 516 us -> 305 us (0.59)
  waiting for transfers between devices: 372 us -> 74.1 us
  Pallas kernels: 0 us -> 95.6 us
  starting transfers between devices: 0.38 us -> 59.7 us
  matrix products: 76.3 us -> 34.2 us
  blocking collectives: 23.9 us -> 0 us
  between operations: 13.9 us -> 1.58 us
  local copies, waits for them, and re-layouts: 6.61 us -> 18.6 us
    psum x1 -> x0, waiting for transfers between devices: 188 us -> none  [per_device(): d_norm = lax.psum(d_part, 'hidden')]
    reduce_scatter x2 -> x0, waiting for transfers between devices: 128 us -> none  [the longest x1 73.9 us: per_device(): lax.psum_scatter(down_part, 'width', scatter_dimension=0, tiled=True)]
    pallas_call x0 -> x18, Pallas kernels: none -> 95.6 us  [the longest x2 35 us: project(): call(functools.partial(kernel, pieces), (steps,), 1, [anywhere] + specs +...]
    ppermute x0 -> x63, waiting for transfers between devices: none -> 74.1 us  [swap(): return lax.ppermute(value, axis, [(i, i ^ mask) for i in range(size)])]
    ppermute x0 -> x63, starting transfers between devices: none -> 59.7 us  [swap(): return lax.ppermute(value, axis, [(i, i ^ mask) for i in range(size)])]
    all_gather x2 -> x0, waiting for transfers between devices: 55.5 us -> none  [the longest x1 33.6 us: per_device(): lax.all_gather(pre_grad.astype(jnp.bfloat16), 'width', axis=0, tiled=True)]
    dot_general x14 -> x5, matrix products: 76.3 us -> 34.2 us  [the longest x3 32.6 us: mm(): lax.dot_general(a, b, (dims, ((), ())), preferred_element_type=jnp.float32)]
    psum x2 -> x0, blocking collectives: 23.9 us -> none  [the longest x1 12.7 us: per_device(): lax.psum((jnp.sum(x_full, 1), jnp.sum(x_full * x_full, 1)), 'width')]
  transfers between devices with their start and end apart: 5 -> 63, of which waited for: 5 -> 13; matrix products, arithmetic and copies ran while one was open for 9% -> 20% of each run, Pallas kernels for 0% -> 22%
where the time goes in v1:
time: 305 us; the launch traced here: 304 us
  Pallas kernels  95.6 us (31%)
  waiting for transfers between devices  74.1 us (24%)
  starting transfers between devices  59.7 us (20%)
  matrix products  34.2 us (11%)
  other arithmetic  20.3 us (7%)
  local copies, waits for them, and re-layouts  18.6 us (6%)
    ppermute x63, waiting for transfers between devices, swap(): return lax.ppermute(value, axis, [(i, i ^ mask) for i in range(size)])  74.1 us
    ppermute x63, starting transfers between devices, swap(): return lax.ppermute(value, axis, [(i, i ^ mask) for i in range(size)])  59.7 us
    pallas_call x2, Pallas kernels, project(): call(functools.partial(kernel, pieces), (steps,), 1, [anywhere] + specs +...  35 us
    dot_general x3, matrix products, mm(): lax.dot_general(a, b, (dims, ((), ())), preferred_element_type=jnp.float32)  32.6 us
    pallas_call x4, Pallas kernels, part(): call(functools.partial(part_kernel, not buffers), (dw // cols,), 1, [anyw...  28.9 us
    pallas_call x4, Pallas kernels, mid(): call(mid_kernel, (half // TILE,), 0, [anywhere] + [rows_spec(fh)] * 4 + [...  15 us
    pallas_call x4, Pallas kernels, norm_a(): call(norm_a_kernel, (1,), 1, [anywhere, plain(rows, dw), plain(rows, dw),...  8.47 us
    pallas_call x4, Pallas kernels, norm_b(): call(functools.partial(norm_b_kernel, dim), (1,), 1, [anywhere, plain(row...  8.24 us
  transfers between devices with their start and end apart: 63, of which 13 were waited for; matrix products, arithmetic and copies ran while one was open for 20% of the time, Pallas kernels for 22%

profile of v1, /device:TPU:0, one launch (start us, length us, event | category | flops | bytes accessed | tf_op | source)
XLA Modules:
  0.0 304.0 jit_solution(4465148618555686106)
XLA Ops:
  0.7 2.8 convert_reduce_fusion
  4.1 2.6 collective-permute-start.3
  9.4 17.1 %shard_map.137 = (bf16[1152,1280]{1,0:T(8,128)(2,1)}, bf16[1152,1280]{1,0:T(8,128)(2,1)}, bf16[1152,128]{1,0:T(8,128)(2,1)}, bf16[192,1728]{1,0:T(8,128)(2,1)}, ...) custom-call(s32[18]{0:T(128)} %broadcast_select_fusion.order, ...), custom_call_target="tpu_custom_call" | custom-call | flops 5096079360 | bytes 17252352 | tf_op jit(solution)/shard_map/pallas_call | solution.py:258
  31.2 17.8 %shard_map.138 = (bf16[1152,1280]{1,0:T(8,128)(2,1)}, bf16[192,1728]{1,0:T(8,128)(2,1)}, bf16[192,1728]{1,0:T(8,128)(2,1)}, bf16[192,1728]{1,0:T(8,128)(2,1)}, b...) custom-call(s32[18]{0:T(128)} %broadcast_select_fusion.order, ...), custom_call_target="tpu_custom_call" | custom-call | flops 5096079360 | bytes 17252352 | tf_op jit(solution)/shard_map/pallas_call | solution.py:258
  50.4 1.9 collective-permute-start.11
  52.8 1.3 add_convert_fusion.2.us
  58.7 10.0 %collective-permute-done.11.dr = bf16[192,1728]{1,0:T(8,128)(2,1)S(1)} collective-permute-done((bf16[192,1728]{1,0:T(8,128)(2,1)S(1)}, bf16[192,1728]{1,0:T(8,128)(2,1)S(1)}, u32[]{:S(2)}, u32[]{:S(2)}) %collective-permute-start.11) | collective-permute-done | bytes 663584 | tf_op jit(solution)/shard_map/ppermute | solution.py:42
  69.5 13.4 %collective-permute-done.12.ur = bf16[192,1728]{1,0:T(8,128)(2,1)} collective-permute-done((bf16[192,1728]{1,0:T(8,128)(2,1)S(1)}, bf16[192,1728]{1,0:T(8,128)(2,1)}, u32[]{:S(2)}, u32[]{:S(2)}) %collective-permute-start.12) | collective-permute-done | bytes 663584 | tf_op jit(solution)/shard_map/ppermute | solution.py:42
  82.9 4.6 %shard_map.139 = (bf16[2,192,1728]{2,1,0:T(8,128)(2,1)}, f32[1,1728]{1,0:T(1,128)}) custom-call(bf16[64,1728]{1,0:T(8,128)(2,1)} %add_convert_fusion.6.dep.us, bf16[192,1728]{1,0:T(8,128)(2,1)} %copy-done.5, bf16[192,1728]{1,0:T(8,128)(2,1)} %copy-done.19, bf16[192,1728]{1,0:T(8,128)(2,1)} %copy-done.7, bf16[192,1728]{1,0:T(8,128)(2,1)} %collective-permute-done.12.ur, ...), custom_call_target="tpu_custom_call" | custom-call | flops 9953280 | bytes 3981312 | tf_op jit(solution)/shard_map/pallas_call | solution.py:317
  87.5 1.8 collective-permute-start.16
  89.6 1.4 collective-permute-done.13.oth
  91.0 8.0 %shard_map.140 = (bf16[192,1280]{1,0:T(8,128)(2,1)}, bf16[192,1280]{1,0:T(8,128)(2,1)}, bf16[1152,1728]{1,0:T(8,128)(2,1)}, bf16[1152,1728]{1,0:T(8,128)(2,1)}) custom-call(s32[1]{0:T(128)} %bitcast.1.flags, f32[1,1728]{1,0:T(1,128)} %get-tuple-element.148.dep, bf16[2,192,1728]{2,1,0:T(8,128)(2,1)} %get-tuple-element.149.own, ...), custom_call_target="tpu_custom_call" | custom-call | flops 1698693120 | bytes 10715136 | tf_op jit(solution)/shard_map/pallas_call | solution.py:334
  99.0 1.8 collective-permute-start.14
  100.8 5.1 %collective-permute-done.16.ur = bf16[192,1728]{1,0:T(8,128)(2,1)S(1)} collective-permute-done((bf16[192,1728]{1,0:T(8,128)(2,1)S(1)}, bf16[192,1728]{1,0:T(8,128)(2,1)S(1)}, u32[]{:S(2)}, u32[]{:S(2)}) %collective-permute-start.16) | collective-permute-done | bytes 663584 | tf_op jit(solution)/shard_map/ppermute | solution.py:42
  105.9 14.3 %collective-permute-done.15.dr = bf16[192,1728]{1,0:T(8,128)(2,1)} collective-permute-done((bf16[192,1728]{1,0:T(8,128)(2,1)S(1)}, bf16[192,1728]{1,0:T(8,128)(2,1)}, u32[]{:S(2)}, u32[]{:S(2)}) %collective-permute-start.15) | collective-permute-done | bytes 663584 | tf_op jit(solution)/shard_map/ppermute | solution.py:42
  120.2 4.6 %shard_map.141 = (bf16[2,192,1728]{2,1,0:T(8,128)(2,1)}, f32[1,1728]{1,0:T(1,128)}) custom-call(bf16[192,1280]{1,0:T(8,128)(2,1)} %get-tuple-element.153.dep, bf16[192,1728]{1,0:T(8,128)(2,1)} %copy-done.4, bf16[192,1728]{1,0:T(8,128)(2,1)} %collective-permute-done.15.dr, bf16[192,1728]{1,0:T(8,128)(2,1)} %copy-done.6, bf16[192,1728]{1,0:T(8,128)(2,1)} %copy-done.21, ...), custom_call_target="tpu_custom_call" | custom-call | flops 9953280 | bytes 3981312 | tf_op jit(solution)/shard_map/pallas_call | solution.py:317
  124.9 1.8 collective-permute-start.21
  128.2 1.9 collective-permute-start.19
  131.2 8.0 %shard_map.142 = (bf16[192,1280]{1,0:T(8,128)(2,1)}, bf16[192,1280]{1,0:T(8,128)(2,1)}, bf16[1152,1728]{1,0:T(8,128)(2,1)}, bf16[1152,1728]{1,0:T(8,128)(2,1)}) custom-call(s32[1]{0:T(128)} %bitcast.1.flags, bf16[96,1280]{1,0:T(8,128)(2,1)} %copy-done.15, ...), custom_call_target="tpu_custom_call", output_to_operand_aliasing={{2}: (5, {}), {3}: (6, {})} | custom-call | flops 1698693120 | bytes 10715136 | tf_op jit(solution)/shard_map/pallas_call | solution.py:334
  141.0 6.7 %collective-permute-done.20.dr = bf16[128,1728]{1,0:T(8,128)(2,1)} collective-permute-done((bf16[128,1728]{1,0:T(8,128)(2,1)S(1)}, bf16[128,1728]{1,0:T(8,128)(2,1)}, u32[]{:S(2)}, u32[]{:S(2)}) %collective-permute-start.20) | collective-permute-done | bytes 442400 | tf_op jit(solution)/shard_map/ppermute | solution.py:42
  147.7 3.0 shard_map.143
  150.7 2.2 copy.38
  152.9 1.7 collective-permute-start.22
  154.9 1.7 collective-permute-start.18
  156.6 2.6 collective-permute-start.25
  159.3 2.1 collective-permute-done.22.dr
  161.4 4.5 %collective-permute-done.23.ur = bf16[64,1728]{1,0:T(8,128)(2,1)S(1)} collective-permute-done((bf16[64,1728]{1,0:T(8,128)(2,1)S(1)}, bf16[64,1728]{1,0:T(8,128)(2,1)S(1)}, u32[]{:S(2)}, u32[]{:S(2)}) %collective-permute-start.23) | collective-permute-done | bytes 221216 | tf_op jit(solution)/shard_map/ppermute | solution.py:42
  166.5 2.8 shard_map.144
  172.0 1.3 copy.39.oth
  173.3 7.0 %shard_map.145 = (bf16[128,1280]{1,0:T(8,128)(2,1)}, bf16[128,1280]{1,0:T(8,128)(2,1)}, bf16[1152,1728]{1,0:T(8,128)(2,1)}, bf16[1152,1728]{1,0:T(8,128)(2,1)}) custom-call(s32[1]{0:T(128)} %bitcast.1.flags, f32[1,1728]{1,0:T(1,128)} %get-tuple-element.163.dep, ...), custom_call_target="tpu_custom_call", output_to_operand_aliasing={{2}: (5, {}), {3}: (6, {})} | custom-call | flops 1132462080 | bytes 8617984 | tf_op jit(solution)/shard_map/pallas_call | solution.py:334
  181.8 2.2 shard_map.146
  184.1 1.7 collective-permute-start.28
  185.9 1.8 collective-permute-start.33
  187.8 1.6 collective-permute-start.32
  189.3 5.9 %shard_map.147 = (bf16[64,1280]{1,0:T(8,128)(2,1)}, bf16[64,1280]{1,0:T(8,128)(2,1)}, bf16[1152,1728]{1,0:T(8,128)(2,1)}, bf16[1152,1728]{1,0:T(8,128)(2,1)}) custom-call(s32[1]{0:T(128)} %bitcast.1.flags, f32[48,128]{1,0:T(8,128)} %get-tuple-element.170.dep, ...), custom_call_target="tpu_custom_call", output_to_operand_aliasing={{2}: (5, {}), {3}: (6, {})} | custom-call | flops 566231040 | bytes 6520832 | tf_op jit(solution)/shard_map/pallas_call | solution.py:334
  196.5 2.2 shard_map.148
  198.7 2.6 collective-permute-start.30
  203.2 1.6 collective-permute-start.35
  204.9 10.8 %fusion.2 = f32[16,1280]{1,0:T(8,128)S(1)} fusion(bf16[1152,1728]{1,0:T(8,128)(2,1)} %get-tuple-element.194, bf16[1728,1280]{1,0:T(8,128)(2,1)} %w.1, bf16[1152,1280]{1,0:T(8,128)(2,1)} %get-tuple-element.176, bf16[1152,128]{1,0:T(8,128)(2,1)} %get-tuple-element.175), kind=kOutput, calls=%fused_computation.6 | convolution fusion | flops 5147688960 | bytes 11730944 | tf_op jit(solution)/shard_map/dot_general | solution.py:71
  217.7 2.2 shard_map.149
  219.9 1.5 collective-permute-start.41
  222.5 2.6 collective-permute-start.39
  225.1 10.9 %fusion.26 = f32[1728,1280]{1,0:T(8,128)} fusion(bf16[1152,1728]{1,0:T(8,128)(2,1)} %get-tuple-element.194, bf16[1152,1280]{1,0:T(8,128)(2,1)} %get-tuple-element.195), kind=kOutput, calls=%fused_computation.109 | convolution fusion | flops 5096079360 | bytes 15777792 | tf_op jit(solution)/shard_map/dot_general | solution.py:71
  239.1 2.1 shard_map.150
  241.1 2.2 shard_map.151.dep
  243.9 2.0 shard_map.152
  245.9 1.5 collective-permute-start.48
  248.1 1.5 collective-permute-start.45
  250.7 2.6 collective-permute-start.52
  253.4 1.3 collective-permute-start.38
  254.7 1.3 add_add_fusion.5.sums
  257.3 2.0 shard_map.153.dep
  259.7 1.9 shard_map.154
  261.5 2.6 collective-permute-start.50
  264.2 1.7 collective-permute-start.55
  265.8 10.9 %fusion.27 = f32[1728,1280]{1,0:T(8,128)} fusion(bf16[1152,1728]{1,0:T(8,128)(2,1)} %get-tuple-element.203, bf16[1152,1280]{1,0:T(8,128)(2,1)} %get-tuple-element.204), kind=kOutput, calls=%fused_computation.110 | convolution fusion | flops 5096079360 | bytes 15777792 | tf_op jit(solution)/shard_map/dot_general | solution.py:71
  277.3 1.7 collective-permute-start.53
  279.6 1.4 collective-permute-start.56
  281.0 2.9 collective-permute-done.54
  284.0 1.4 collective-permute-start.57
  285.7 1.4 collective-permute-start.58
  287.1 1.7 collective-permute-done.61
  289.6 11.3 %collective-permute-done.62 = f32[3,16,1280]{2,1,0:T(8,128)S(1)} collective-permute-done((f32[3,16,1280]{2,1,0:T(8,128)S(1)}, f32[3,16,1280]{2,1,0:T(8,128)S(1)}, u32[]{:S(2)}, u32[]{:S(2)}) %collective-permute-start.62) | collective-permute-done | bytes 245792 | tf_op jit(solution)/shard_map/ppermute | solution.py:42
  302.4 1.6 copy-done.3
  (271 shorter events, 41.8 us)
Async XLA Ops:
  3.6 24.2 %collective-permute-start.2 = (f32[2,1152]{1,0:T(2,128)S(1)}, f32[2,1152]{1,0:T(2,128)S(1)}, u32[]{:S(2)}, u32[]{:S(2)}) collective-permute-start(f32[2,1152]{1,0:T(2,128)S(1)} %pad_maximum_fusion.4.dep), channel_id=1, source_target_pairs={{0,8},{8,0},{16,24},{24,16},{1,9},{9,1},{17,25},{25,17},{2,10},{10... | collective-permute-start | bytes 27656 | tf_op jit(solution)/shard_map/ppermute | solution.py:42
  4.1 23.7 %collective-permute-start.3 = (f32[2,1152]{1,0:T(2,128)S(1)}, f32[2,1152]{1,0:T(2,128)S(1)}, u32[]{:S(2)}, u32[]{:S(2)}) collective-permute-start(f32[2,1152]{1,0:T(2,128)S(1)} %pad_maximum_fusion.4.dep), channel_id=1, source_target_pairs={{0,16},{8,24},{16,0},{24,8},{1,17},{9,25},{17,1},{25,9},{2,18},{10... | collective-permute-start | bytes 27656 | tf_op jit(solution)/shard_map/ppermute | solution.py:42
  6.7 21.1 %collective-permute-start.4 = (f32[2,1152]{1,0:T(2,128)S(1)}, f32[2,1152]{1,0:T(2,128)S(1)}, u32[]{:S(2)}, u32[]{:S(2)}) collective-permute-start(f32[2,1152]{1,0:T(2,128)S(1)} %pad_maximum_fusion.4.dep), channel_id=1, source_target_pairs={{0,24},{8,16},{16,8},{24,0},{1,25},{9,17},{17,9},{25,1},{2,26},{10... | collective-permute-start | bytes 27656 | tf_op jit(solution)/shard_map/ppermute | solution.py:42
  26.6 2.4 collective-permute-start.1
  26.8 3.5 %collective-permute-start = (bf16[64,1728]{1,0:T(8,128)(2,1)}, bf16[64,1728]{1,0:T(8,128)(2,1)S(1)}, u32[]{:S(2)}, u32[]{:S(2)}) collective-permute-start(bf16[64,1728]{1,0:T(8,128)(2,1)} %get-tuple-element.117), channel_id=1, source_target_pairs={{0,8},{8,0},{16,24},{24,16},{1,9},{9,1},{17,25},{25,17},{2,10},{10... | collective-permute-start | bytes 663560 | tf_op jit(solution)/shard_map/ppermute | solution.py:42
  49.0 3.3 %collective-permute-start.10 = (bf16[192,1728]{1,0:T(8,128)(2,1)}, bf16[192,1728]{1,0:T(8,128)(2,1)S(1)}, u32[]{:S(2)}, u32[]{:S(2)}) collective-permute-start(bf16[192,1728]{1,0:T(8,128)(2,1)} %get-tuple-element.135), channel_id=1, source_target_pairs={{0,8},{8,0},{16,24},{24,16},{1,9},{9,1},{17,25},{25,17},{2,10},{10... | collective-permute-start | bytes 1990664 | tf_op jit(solution)/shard_map/ppermute | solution.py:42
  49.3 4.9 %collective-permute-start.9 = (bf16[192,1728]{1,0:T(8,128)(2,1)S(1)}, bf16[192,1728]{1,0:T(8,128)(2,1)S(1)}, u32[]{:S(2)}, u32[]{:S(2)}) collective-permute-start(bf16[192,1728]{1,0:T(8,128)(2,1)S(1)} %copy-done.52), channel_id=1, source_target_pairs={{0,8},{8,0},{16,24},{24,16},{1,9},{9,1},{17,25},{25,17},{2,10},{10... | collective-permute-start | bytes 1990664 | tf_op jit(solution)/shard_map/ppermute | solution.py:42
  49.6 6.4 %collective-permute-start.7 = (bf16[128,1728]{1,0:T(8,128)(2,1)}, bf16[128,1728]{1,0:T(8,128)(2,1)S(1)}, u32[]{:S(2)}, u32[]{:S(2)}) collective-permute-start(bf16[128,1728]{1,0:T(8,128)(2,1)} %get-tuple-element.129), channel_id=1, source_target_pairs={{0,8},{8,0},{16,24},{24,16},{1,9},{9,1},{17,25},{25,17},{2,10},{10... | collective-permute-start | bytes 1327112 | tf_op jit(solution)/shard_map/ppermute | solution.py:42
  50.4 18.3 %collective-permute-start.11 = (bf16[192,1728]{1,0:T(8,128)(2,1)S(1)}, bf16[192,1728]{1,0:T(8,128)(2,1)S(1)}, u32[]{:S(2)}, u32[]{:S(2)}) collective-permute-start(bf16[192,1728]{1,0:T(8,128)(2,1)S(1)} %add_convert_fusion.3.ds), channel_id=1, source_target_pairs={{0,16},{8,24},{16,0},{24,8},{1,17},{9,25},{17,1},{25,9},{2,18},{10... | collective-permute-start | bytes 1990664 | tf_op jit(solution)/shard_map/ppermute | solution.py:42
  52.3 2.4 collective-permute-start.8
  52.3 4.7 %collective-permute-start.6 = (bf16[128,1728]{1,0:T(8,128)(2,1)}, bf16[128,1728]{1,0:T(8,128)(2,1)S(1)}, u32[]{:S(2)}, u32[]{:S(2)}) collective-permute-start(bf16[128,1728]{1,0:T(8,128)(2,1)} %get-tuple-element.127), channel_id=1, source_target_pairs={{0,8},{8,0},{16,24},{24,16},{1,9},{9,1},{17,25},{25,17},{2,10},{10... | collective-permute-start | bytes 1327112 | tf_op jit(solution)/shard_map/ppermute | solution.py:42
  54.2 3.7 %collective-permute-start.5 = (bf16[64,1728]{1,0:T(8,128)(2,1)}, bf16[64,1728]{1,0:T(8,128)(2,1)S(1)}, u32[]{:S(2)}, u32[]{:S(2)}) collective-permute-start(bf16[64,1728]{1,0:T(8,128)(2,1)} %get-tuple-element.125), channel_id=1, source_target_pairs={{0,8},{8,0},{16,24},{24,16},{1,9},{9,1},{17,25},{25,17},{2,10},{10... | collective-permute-start | bytes 663560 | tf_op jit(solution)/shard_map/ppermute | solution.py:42
  54.4 34.9 %copy-start.4 = (bf16[192,1728]{1,0:T(8,128)(2,1)}, bf16[192,1728]{1,0:T(8,128)(2,1)S(1)}, u32[]{:S(2)}) copy-start(bf16[192,1728]{1,0:T(8,128)(2,1)S(1)} %add_convert_fusion.1.ds) | copy-start | bytes 1990660
  54.7 28.2 %collective-permute-start.12 = (bf16[192,1728]{1,0:T(8,128)(2,1)S(1)}, bf16[192,1728]{1,0:T(8,128)(2,1)}, u32[]{:S(2)}, u32[]{:S(2)}) collective-permute-start(bf16[192,1728]{1,0:T(8,128)(2,1)S(1)} %add_convert_fusion.2.us), channel_id=1, source_target_pairs={{0,16},{8,24},{16,0},{24,8},{1,17},{9,25},{17,1},{25,9},{2,18},{10... | collective-permute-start | bytes 1990664 | tf_op jit(solution)/shard_map/ppermute | solution.py:42
  87.5 3.5 %collective-permute-start.13 = (bf16[2,192,1728]{2,1,0:T(8,128)(2,1)}, bf16[2,192,1728]{2,1,0:T(8,128)(2,1)}, u32[]{:S(2)}, u32[]{:S(2)}) collective-permute-start(bf16[2,192,1728]{2,1,0:T(8,128)(2,1)} %get-tuple-element.149.own), channel_id=1, source_target_pairs={{0,8},{8,0},{16,24},{24,16},{1,9},{9,1},{17,25},{25,17},{2,10},{10... | collective-permute-start | bytes 3981320 | tf_op jit(solution)/shard_map/ppermute | solution.py:42
  87.5 18.4 %collective-permute-start.16 = (bf16[192,1728]{1,0:T(8,128)(2,1)S(1)}, bf16[192,1728]{1,0:T(8,128)(2,1)S(1)}, u32[]{:S(2)}, u32[]{:S(2)}) collective-permute-start(bf16[192,1728]{1,0:T(8,128)(2,1)S(1)} %add_convert_fusion.us), channel_id=1, source_target_pairs={{0,16},{8,24},{16,0},{24,8},{1,17},{9,25},{17,1},{25,9},{2,18},{10... | collective-permute-start | bytes 1990664 | tf_op jit(solution)/shard_map/ppermute | solution.py:42
  89.3 30.9 %collective-permute-start.15 = (bf16[192,1728]{1,0:T(8,128)(2,1)S(1)}, bf16[192,1728]{1,0:T(8,128)(2,1)}, u32[]{:S(2)}, u32[]{:S(2)}) collective-permute-start(bf16[192,1728]{1,0:T(8,128)(2,1)S(1)} %add_convert_fusion.1.ds), channel_id=1, source_target_pairs={{0,16},{8,24},{16,0},{24,8},{1,17},{9,25},{17,1},{25,9},{2,18},{10... | collective-permute-start | bytes 1990664 | tf_op jit(solution)/shard_map/ppermute | solution.py:42
  99.0 28.0 %collective-permute-start.14 = (bf16[192,1280]{1,0:T(8,128)(2,1)}, bf16[192,1280]{1,0:T(8,128)(2,1)}, u32[]{:S(2)}, u32[]{:S(2)}) collective-permute-start(bf16[192,1280]{1,0:T(8,128)(2,1)} %get-tuple-element.151), channel_id=1, source_target_pairs={{0,1},{1,0},{2,3},{3,2},{4,5},{5,4},{6,7},{7,6},{8,9},{9,8},{10,11... | collective-permute-start | bytes 1474568 | tf_op jit(solution)/shard_map/ppermute | solution.py:42
  124.8 5.3 %collective-permute-start.17 = (bf16[2,192,1728]{2,1,0:T(8,128)(2,1)}, bf16[2,192,1728]{2,1,0:T(8,128)(2,1)S(1)}, u32[]{:S(2)}, u32[]{:S(2)}) collective-permute-start(bf16[2,192,1728]{2,1,0:T(8,128)(2,1)} %get-tuple-element.155.own), channel_id=1, source_target_pairs={{0,8},{8,0},{16,24},{24,16},{1,9},{9,1},{17,25},{25,17},{2,10},{10... | collective-permute-start | bytes 3981320 | tf_op jit(solution)/shard_map/ppermute | solution.py:42
  124.9 16.1 %collective-permute-start.21 = (bf16[128,1728]{1,0:T(8,128)(2,1)S(1)}, bf16[128,1728]{1,0:T(8,128)(2,1)}, u32[]{:S(2)}, u32[]{:S(2)}) collective-permute-start(bf16[128,1728]{1,0:T(8,128)(2,1)S(1)} %copy-done.11), channel_id=1, source_target_pairs={{0,16},{8,24},{16,0},{24,8},{1,17},{9,25},{17,1},{25,9},{2,18},{10... | collective-permute-start | bytes 1327112 | tf_op jit(solution)/shard_map/ppermute | solution.py:42
  126.7 21.0 %collective-permute-start.20 = (bf16[128,1728]{1,0:T(8,128)(2,1)S(1)}, bf16[128,1728]{1,0:T(8,128)(2,1)}, u32[]{:S(2)}, u32[]{:S(2)}) collective-permute-start(bf16[128,1728]{1,0:T(8,128)(2,1)S(1)} %copy-done.10), channel_id=1, source_target_pairs={{0,16},{8,24},{16,0},{24,8},{1,17},{9,25},{17,1},{25,9},{2,18},{10... | collective-permute-start | bytes 1327112 | tf_op jit(solution)/shard_map/ppermute | solution.py:42
  128.2 11.0 %collective-permute-start.19 = (bf16[96,1280]{1,0:T(8,128)(2,1)S(1)}, bf16[96,1280]{1,0:T(8,128)(2,1)}, u32[]{:S(2)}, u32[]{:S(2)}) collective-permute-start(bf16[96,1280]{1,0:T(8,128)(2,1)S(1)} %fusion.4.dep), channel_id=1, source_target_pairs={{0,2},{1,3},{2,0},{3,1},{4,6},{5,7},{6,4},{7,5},{8,10},{9,11},{10,... | collective-permute-start | bytes 737288 | tf_op jit(solution)/shard_map/ppermute | solution.py:42
  152.9 19.1 %collective-permute-start.24 = (bf16[2,128,1728]{1,2,0:T(8,128)(2,1)}, bf16[2,128,1728]{1,2,0:T(8,128)(2,1)S(1)}, u32[]{:S(2)}, u32[]{:S(2)}) collective-permute-start(bf16[2,128,1728]{1,2,0:T(8,128)(2,1)} %copy.38), channel_id=1, source_target_pairs={{0,8},{8,0},{16,24},{24,16},{1,9},{9,1},{17,25},{25,17},{2,10},{10... | collective-permute-start | bytes 2654216 | tf_op jit(solution)/shard_map/ppermute | solution.py:42
  152.9 8.5 %collective-permute-start.22 = (bf16[64,1728]{1,0:T(8,128)(2,1)S(1)}, bf16[64,1728]{1,0:T(8,128)(2,1)S(1)}, u32[]{:S(2)}, u32[]{:S(2)}) collective-permute-start(bf16[64,1728]{1,0:T(8,128)(2,1)S(1)} %copy-done.16), channel_id=1, source_target_pairs={{0,16},{8,24},{16,0},{24,8},{1,17},{9,25},{17,1},{25,9},{2,18},{10... | collective-permute-start | bytes 663560 | tf_op jit(solution)/shard_map/ppermute | solution.py:42
  154.6 11.2 %collective-permute-start.23 = (bf16[64,1728]{1,0:T(8,128)(2,1)S(1)}, bf16[64,1728]{1,0:T(8,128)(2,1)S(1)}, u32[]{:S(2)}, u32[]{:S(2)}) collective-permute-start(bf16[64,1728]{1,0:T(8,128)(2,1)S(1)} %copy-done.8), channel_id=1, source_target_pairs={{0,16},{8,24},{16,0},{24,8},{1,17},{9,25},{17,1},{25,9},{2,18},{10... | collective-permute-start | bytes 663560 | tf_op jit(solution)/shard_map/ppermute | solution.py:42
  154.9 25.4 %collective-permute-start.18 = (bf16[192,1280]{1,0:T(8,128)(2,1)}, bf16[192,1280]{1,0:T(8,128)(2,1)S(1)}, u32[]{:S(2)}, u32[]{:S(2)}) collective-permute-start(bf16[192,1280]{1,0:T(8,128)(2,1)} %get-tuple-element.159), channel_id=1, source_target_pairs={{0,1},{1,0},{2,3},{3,2},{4,5},{5,4},{6,7},{7,6},{8,9},{9,8},{10,11... | collective-permute-start | bytes 1474568 | tf_op jit(solution)/shard_map/ppermute | solution.py:42
  156.6 24.5 %collective-permute-start.25 = (bf16[48,1280]{1,0:T(8,128)(2,1)S(1)}, bf16[48,1280]{1,0:T(8,128)(2,1)S(1)}, u32[]{:S(2)}, u32[]{:S(2)}) collective-permute-start(bf16[48,1280]{1,0:T(8,128)(2,1)S(1)} %copy-done.23), channel_id=1, source_target_pairs={{0,4},{1,5},{2,6},{3,7},{4,0},{5,1},{6,2},{7,3},{8,12},{9,13},{10,... | collective-permute-start | bytes 368648 | tf_op jit(solution)/shard_map/ppermute | solution.py:42
  170.1 1.3 collective-permute-start.59
  170.9 16.8 %collective-permute-start.26 = (bf16[2,64,1728]{2,1,0:T(8,128)(2,1)}, bf16[2,64,1728]{2,1,0:T(8,128)(2,1)S(1)}, u32[]{:S(2)}, u32[]{:S(2)}) collective-permute-start(bf16[2,64,1728]{2,1,0:T(8,128)(2,1)} %get-tuple-element.171.own), channel_id=1, source_target_pairs={{0,8},{8,0},{16,24},{24,16},{1,9},{9,1},{17,25},{25,17},{2,10},{10... | collective-permute-start | bytes 1327112 | tf_op jit(solution)/shard_map/ppermute | solution.py:42
  184.0 11.2 %collective-permute-start.27 = (f32[48,128]{1,0:T(8,128)}, f32[48,128]{1,0:T(8,128)S(1)}, u32[]{:S(2)}, u32[]{:S(2)}) collective-permute-start(f32[48,128]{1,0:T(8,128)} %get-tuple-element.170.dep), channel_id=1, source_target_pairs={{0,8},{8,0},{16,24},{24,16},{1,9},{9,1},{17,25},{25,17},{2,10},{10... | collective-permute-start | bytes 73736 | tf_op jit(solution)/shard_map/ppermute | solution.py:42
  184.1 11.8 %collective-permute-start.28 = (f32[48,128]{1,0:T(8,128)}, f32[48,128]{1,0:T(8,128)S(1)}, u32[]{:S(2)}, u32[]{:S(2)}) collective-permute-start(f32[48,128]{1,0:T(8,128)} %get-tuple-element.170.dep), channel_id=1, source_target_pairs={{0,16},{8,24},{16,0},{24,8},{1,17},{9,25},{17,1},{25,9},{2,18},{10... | collective-permute-start | bytes 73736 | tf_op jit(solution)/shard_map/ppermute | solution.py:42
  185.9 10.1 %collective-permute-start.29 = (f32[48,128]{1,0:T(8,128)}, f32[48,128]{1,0:T(8,128)S(1)}, u32[]{:S(2)}, u32[]{:S(2)}) collective-permute-start(f32[48,128]{1,0:T(8,128)} %get-tuple-element.170.dep), channel_id=1, source_target_pairs={{0,24},{8,16},{16,8},{24,0},{1,25},{9,17},{17,9},{25,1},{2,26},{10... | collective-permute-start | bytes 73736 | tf_op jit(solution)/shard_map/ppermute | solution.py:42
  185.9 15.5 %collective-permute-start.33 = (bf16[96,1280]{1,0:T(8,128)(2,1)S(1)}, bf16[96,1280]{1,0:T(8,128)(2,1)S(1)}, u32[]{:S(2)}, u32[]{:S(2)}) collective-permute-start(bf16[96,1280]{1,0:T(8,128)(2,1)S(1)} %copy-done.14), channel_id=1, source_target_pairs={{0,2},{1,3},{2,0},{3,1},{4,6},{5,7},{6,4},{7,5},{8,10},{9,11},{10,... | collective-permute-start | bytes 737288 | tf_op jit(solution)/shard_map/ppermute | solution.py:42
  187.8 14.8 %collective-permute-start.32 = (bf16[128,1280]{1,0:T(8,128)(2,1)S(1)}, bf16[128,1280]{1,0:T(8,128)(2,1)S(1)}, u32[]{:S(2)}, u32[]{:S(2)}) collective-permute-start(bf16[128,1280]{1,0:T(8,128)(2,1)S(1)} %copy-done.53), channel_id=1, source_target_pairs={{0,1},{1,0},{2,3},{3,2},{4,5},{5,4},{6,7},{7,6},{8,9},{9,8},{10,11... | collective-permute-start | bytes 983048 | tf_op jit(solution)/shard_map/ppermute | solution.py:42
  195.2 8.0 %collective-permute-start.31 = (bf16[64,1280]{1,0:T(8,128)(2,1)}, bf16[64,1280]{1,0:T(8,128)(2,1)S(1)}, u32[]{:S(2)}, u32[]{:S(2)}) collective-permute-start(bf16[64,1280]{1,0:T(8,128)(2,1)} %get-tuple-element.178), channel_id=1, source_target_pairs={{0,1},{1,0},{2,3},{3,2},{4,5},{5,4},{6,7},{7,6},{8,9},{9,8},{10,11... | collective-permute-start | bytes 491528 | tf_op jit(solution)/shard_map/ppermute | solution.py:42
  198.7 17.0 %collective-permute-start.30 = (bf16[48,1280]{1,0:T(8,128)(2,1)}, bf16[48,1280]{1,0:T(8,128)(2,1)S(1)}, u32[]{:S(2)}, u32[]{:S(2)}) collective-permute-start(bf16[48,1280]{1,0:T(8,128)(2,1)} %shard_map.148), channel_id=1, source_target_pairs={{0,4},{1,5},{2,6},{3,7},{4,0},{5,1},{6,2},{7,3},{8,12},{9,13},{10,... | collective-permute-start | bytes 368648 | tf_op jit(solution)/shard_map/ppermute | solution.py:42
  201.4 15.7 %collective-permute-start.37 = (bf16[48,1280]{1,0:T(8,128)(2,1)S(1)}, bf16[48,1280]{1,0:T(8,128)(2,1)S(1)}, u32[]{:S(2)}, u32[]{:S(2)}) collective-permute-start(bf16[48,1280]{1,0:T(8,128)(2,1)S(1)} %fusion.10), channel_id=1, source_target_pairs={{0,4},{1,5},{2,6},{3,7},{4,0},{5,1},{6,2},{7,3},{8,12},{9,13},{10,... | collective-permute-start | bytes 368648 | tf_op jit(solution)/shard_map/ppermute | solution.py:42
  202.6 13.7 %collective-permute-start.36 = (bf16[64,1280]{1,0:T(8,128)(2,1)S(1)}, bf16[64,1280]{1,0:T(8,128)(2,1)S(1)}, u32[]{:S(2)}, u32[]{:S(2)}) collective-permute-start(bf16[64,1280]{1,0:T(8,128)(2,1)S(1)} %fusion.8), channel_id=1, source_target_pairs={{0,2},{1,3},{2,0},{3,1},{4,6},{5,7},{6,4},{7,5},{8,10},{9,11},{10,... | collective-permute-start | bytes 491528 | tf_op jit(solution)/shard_map/ppermute | solution.py:42
  203.2 13.2 %collective-permute-start.35 = (bf16[32,1280]{1,0:T(8,128)(2,1)S(1)}, bf16[32,1280]{1,0:T(8,128)(2,1)S(1)}, u32[]{:S(2)}, u32[]{:S(2)}) collective-permute-start(bf16[32,1280]{1,0:T(8,128)(2,1)S(1)} %fusion.14), channel_id=1, source_target_pairs={{0,2},{1,3},{2,0},{3,1},{4,6},{5,7},{6,4},{7,5},{8,10},{9,11},{10,... | collective-permute-start | bytes 245768 | tf_op jit(solution)/shard_map/ppermute | solution.py:42
  215.8 21.8 %collective-permute-start.34 = (bf16[96,1280]{1,0:T(8,128)(2,1)S(1)}, bf16[96,1280]{1,0:T(8,128)(2,1)S(1)}, u32[]{:S(2)}, u32[]{:S(2)}) collective-permute-start(bf16[96,1280]{1,0:T(8,128)(2,1)S(1)} %bitcast.149), channel_id=1, source_target_pairs={{0,2},{1,3},{2,0},{3,1},{4,6},{5,7},{6,4},{7,5},{8,10},{9,11},{10,... | collective-permute-start | bytes 737288 | tf_op jit(solution)/shard_map/ppermute | solution.py:42
  219.9 16.7 %collective-permute-start.40 = (f32[48,128]{1,0:T(8,128)}, f32[48,128]{1,0:T(8,128)S(1)}, u32[]{:S(2)}, u32[]{:S(2)}) collective-permute-start(f32[48,128]{1,0:T(8,128)} %get-tuple-element.193), channel_id=1, source_target_pairs={{0,8},{8,0},{16,24},{24,16},{1,9},{9,1},{17,25},{25,17},{2,10},{10... | collective-permute-start | bytes 73736 | tf_op jit(solution)/shard_map/ppermute | solution.py:42
  219.9 17.0 %collective-permute-start.41 = (f32[48,128]{1,0:T(8,128)}, f32[48,128]{1,0:T(8,128)S(1)}, u32[]{:S(2)}, u32[]{:S(2)}) collective-permute-start(f32[48,128]{1,0:T(8,128)} %get-tuple-element.193), channel_id=1, source_target_pairs={{0,16},{8,24},{16,0},{24,8},{1,17},{9,25},{17,1},{25,9},{2,18},{10... | collective-permute-start | bytes 73736 | tf_op jit(solution)/shard_map/ppermute | solution.py:42
  221.5 15.5 %collective-permute-start.42 = (f32[48,128]{1,0:T(8,128)}, f32[48,128]{1,0:T(8,128)S(1)}, u32[]{:S(2)}, u32[]{:S(2)}) collective-permute-start(f32[48,128]{1,0:T(8,128)} %get-tuple-element.193), channel_id=1, source_target_pairs={{0,24},{8,16},{16,8},{24,0},{1,25},{9,17},{17,9},{25,1},{2,26},{10... | collective-permute-start | bytes 73736 | tf_op jit(solution)/shard_map/ppermute | solution.py:42
  222.5 15.9 %collective-permute-start.39 = (bf16[32,1280]{1,0:T(8,128)(2,1)S(1)}, bf16[32,1280]{1,0:T(8,128)(2,1)S(1)}, u32[]{:S(2)}, u32[]{:S(2)}) collective-permute-start(bf16[32,1280]{1,0:T(8,128)(2,1)S(1)} %fusion.15), channel_id=1, source_target_pairs={{0,4},{1,5},{2,6},{3,7},{4,0},{5,1},{6,2},{7,3},{8,12},{9,13},{10,... | collective-permute-start | bytes 245768 | tf_op jit(solution)/shard_map/ppermute | solution.py:42
  236.6 6.7 %collective-permute-start.43 = (bf16[16,1280]{1,0:T(8,128)(2,1)S(1)}, bf16[16,1280]{1,0:T(8,128)(2,1)S(1)}, u32[]{:S(2)}, u32[]{:S(2)}) collective-permute-start(bf16[16,1280]{1,0:T(8,128)(2,1)S(1)} %copy-done.37), channel_id=1, source_target_pairs={{0,4},{1,5},{2,6},{3,7},{4,0},{5,1},{6,2},{7,3},{8,12},{9,13},{10,... | collective-permute-start | bytes 122888 | tf_op jit(solution)/shard_map/ppermute | solution.py:42
  245.9 4.7 %collective-permute-start.47 = (f32[16,128]{1,0:T(8,128)}, f32[16,128]{1,0:T(8,128)S(1)}, u32[]{:S(2)}, u32[]{:S(2)}) collective-permute-start(f32[16,128]{1,0:T(8,128)} %get-tuple-element.199.dep), channel_id=1, source_target_pairs={{0,8},{8,0},{16,24},{24,16},{1,9},{9,1},{17,25},{25,17},{2,10},{10... | collective-permute-start | bytes 24584 | tf_op jit(solution)/shard_map/ppermute | solution.py:42
  245.9 4.8 %collective-permute-start.48 = (f32[16,128]{1,0:T(8,128)}, f32[16,128]{1,0:T(8,128)S(1)}, u32[]{:S(2)}, u32[]{:S(2)}) collective-permute-start(f32[16,128]{1,0:T(8,128)} %get-tuple-element.199.dep), channel_id=1, source_target_pairs={{0,16},{8,24},{16,0},{24,8},{1,17},{9,25},{17,1},{25,9},{2,18},{10... | collective-permute-start | bytes 24584 | tf_op jit(solution)/shard_map/ppermute | solution.py:42
  247.5 5.9 %collective-permute-start.49 = (f32[16,128]{1,0:T(8,128)}, f32[16,128]{1,0:T(8,128)S(1)}, u32[]{:S(2)}, u32[]{:S(2)}) collective-permute-start(f32[16,128]{1,0:T(8,128)} %get-tuple-element.199.dep), channel_id=1, source_target_pairs={{0,24},{8,16},{16,8},{24,0},{1,25},{9,17},{17,9},{25,1},{2,26},{10... | collective-permute-start | bytes 24584 | tf_op jit(solution)/shard_map/ppermute | solution.py:42
  247.8 8.2 %collective-permute-start.44 = (f32[32,128]{1,0:T(8,128)S(1)}, f32[32,128]{1,0:T(8,128)S(1)}, u32[]{:S(2)}, u32[]{:S(2)}) collective-permute-start(f32[32,128]{1,0:T(8,128)S(1)} %copy-done.44), channel_id=1, source_target_pairs={{0,8},{8,0},{16,24},{24,16},{1,9},{9,1},{17,25},{25,17},{2,10},{10... | collective-permute-start | bytes 49160 | tf_op jit(solution)/shard_map/ppermute | solution.py:42
  248.1 8.6 %collective-permute-start.45 = (f32[32,128]{1,0:T(8,128)S(1)}, f32[32,128]{1,0:T(8,128)S(1)}, u32[]{:S(2)}, u32[]{:S(2)}) collective-permute-start(f32[32,128]{1,0:T(8,128)S(1)} %copy-done.44), channel_id=1, source_target_pairs={{0,16},{8,24},{16,0},{24,8},{1,17},{9,25},{17,1},{25,9},{2,18},{10... | collective-permute-start | bytes 49160 | tf_op jit(solution)/shard_map/ppermute | solution.py:42
  250.6 6.1 %collective-permute-start.46 = (f32[32,128]{1,0:T(8,128)S(1)}, f32[32,128]{1,0:T(8,128)S(1)}, u32[]{:S(2)}, u32[]{:S(2)}) collective-permute-start(f32[32,128]{1,0:T(8,128)S(1)} %copy-done.44), channel_id=1, source_target_pairs={{0,24},{8,16},{16,8},{24,0},{1,25},{9,17},{17,9},{25,1},{2,26},{10... | collective-permute-start | bytes 49160 | tf_op jit(solution)/shard_map/ppermute | solution.py:42
  250.7 13.4 %collective-permute-start.52 = (bf16[48,1280]{1,0:T(8,128)(2,1)S(1)}, bf16[48,1280]{1,0:T(8,128)(2,1)S(1)}, u32[]{:S(2)}, u32[]{:S(2)}) collective-permute-start(bf16[48,1280]{1,0:T(8,128)(2,1)S(1)} %copy-done.13), channel_id=1, source_target_pairs={{0,4},{1,5},{2,6},{3,7},{4,0},{5,1},{6,2},{7,3},{8,12},{9,13},{10,... | collective-permute-start | bytes 368648 | tf_op jit(solution)/shard_map/ppermute | solution.py:42
  253.4 35.9 %collective-permute-start.38 = (bf16[192,1280]{1,0:T(8,128)(2,1)S(1)}, bf16[192,1280]{1,0:T(8,128)(2,1)S(1)}, u32[]{:S(2)}, u32[]{:S(2)}) collective-permute-start(bf16[192,1280]{1,0:T(8,128)(2,1)S(1)} %bitcast.128), channel_id=1, source_target_pairs={{0,1},{1,0},{2,3},{3,2},{4,5},{5,4},{6,7},{7,6},{8,9},{9,8},{10,11... | collective-permute-start | bytes 1474568 | tf_op jit(solution)/shard_map/ppermute | solution.py:42
  256.0 22.9 %collective-permute-start.60 = (f32[3,16,1280]{2,1,0:T(8,128)S(1)}, f32[3,16,1280]{2,1,0:T(8,128)S(1)}, u32[]{:S(2)}, u32[]{:S(2)}) collective-permute-start(f32[3,16,1280]{2,1,0:T(8,128)S(1)} %pad_maximum_fusion), channel_id=1, source_target_pairs={{0,1},{1,0},{2,3},{3,2},{4,5},{5,4},{6,7},{7,6},{8,9},{9,8},{10,11... | collective-permute-start | bytes 737288 | tf_op jit(solution)/shard_map/ppermute | solution.py:42
  259.3 17.4 %collective-permute-start.51 = (bf16[32,1280]{1,0:T(8,128)(2,1)}, bf16[32,1280]{1,0:T(8,128)(2,1)S(1)}, u32[]{:S(2)}, u32[]{:S(2)}) collective-permute-start(bf16[32,1280]{1,0:T(8,128)(2,1)} %shard_map.153.dep), channel_id=1, source_target_pairs={{0,4},{1,5},{2,6},{3,7},{4,0},{5,1},{6,2},{7,3},{8,12},{9,13},{10,... | collective-permute-start | bytes 245768 | tf_op jit(solution)/shard_map/ppermute | solution.py:42
  261.5 15.7 %collective-permute-start.50 = (bf16[16,1280]{1,0:T(8,128)(2,1)}, bf16[16,1280]{1,0:T(8,128)(2,1)S(1)}, u32[]{:S(2)}, u32[]{:S(2)}) collective-permute-start(bf16[16,1280]{1,0:T(8,128)(2,1)} %shard_map.154), channel_id=1, source_target_pairs={{0,4},{1,5},{2,6},{3,7},{4,0},{5,1},{6,2},{7,3},{8,12},{9,13},{10,... | collective-permute-start | bytes 122888 | tf_op jit(solution)/shard_map/ppermute | solution.py:42
  264.2 15.3 %collective-permute-start.55 = (bf16[96,1280]{1,0:T(8,128)(2,1)S(1)}, bf16[96,1280]{1,0:T(8,128)(2,1)S(1)}, u32[]{:S(2)}, u32[]{:S(2)}) collective-permute-start(bf16[96,1280]{1,0:T(8,128)(2,1)S(1)} %bitcast.151), channel_id=1, source_target_pairs={{0,2},{1,3},{2,0},{3,1},{4,6},{5,7},{6,4},{7,5},{8,10},{9,11},{10,... | collective-permute-start | bytes 737288 | tf_op jit(solution)/shard_map/ppermute | solution.py:42
  276.8 7.1 %collective-permute-start.54 = (bf16[64,1280]{1,0:T(8,128)(2,1)S(1)}, bf16[64,1280]{1,0:T(8,128)(2,1)S(1)}, u32[]{:S(2)}, u32[]{:S(2)}) collective-permute-start(bf16[64,1280]{1,0:T(8,128)(2,1)S(1)} %bitcast.156), channel_id=1, source_target_pairs={{0,2},{1,3},{2,0},{3,1},{4,6},{5,7},{6,4},{7,5},{8,10},{9,11},{10,... | collective-permute-start | bytes 491528 | tf_op jit(solution)/shard_map/ppermute | solution.py:42
  277.3 8.4 %collective-permute-start.53 = (bf16[32,1280]{1,0:T(8,128)(2,1)S(1)}, bf16[32,1280]{1,0:T(8,128)(2,1)S(1)}, u32[]{:S(2)}, u32[]{:S(2)}) collective-permute-start(bf16[32,1280]{1,0:T(8,128)(2,1)S(1)} %bitcast.161), channel_id=1, source_target_pairs={{0,2},{1,3},{2,0},{3,1},{4,6},{5,7},{6,4},{7,5},{8,10},{9,11},{10,... | collective-permute-start | bytes 245768 | tf_op jit(solution)/shard_map/ppermute | solution.py:42
  279.0 9.8 %collective-permute-start.61 = (f32[3,16,1280]{2,1,0:T(8,128)S(1)}, f32[3,16,1280]{2,1,0:T(8,128)S(1)}, u32[]{:S(2)}, u32[]{:S(2)}) collective-permute-start(f32[3,16,1280]{2,1,0:T(8,128)S(1)} %fusion.25), channel_id=1, source_target_pairs={{0,2},{1,3},{2,0},{3,1},{4,6},{5,7},{6,4},{7,5},{8,10},{9,11},{10,... | collective-permute-start | bytes 737288 | tf_op jit(solution)/shard_map/ppermute | solution.py:42
  279.6 22.6 %collective-permute-start.56 = (bf16[192,1280]{1,0:T(8,128)(2,1)S(1)}, bf16[192,1280]{1,0:T(8,128)(2,1)S(1)}, u32[]{:S(2)}, u32[]{:S(2)}) collective-permute-start(bf16[192,1280]{1,0:T(8,128)(2,1)S(1)} %bitcast.136), channel_id=1, source_target_pairs={{0,1},{1,0},{2,3},{3,2},{4,5},{5,4},{6,7},{7,6},{8,9},{9,8},{10,11... | collective-permute-start | bytes 1474568 | tf_op jit(solution)/shard_map/ppermute | solution.py:42
  284.0 18.2 %collective-permute-start.57 = (bf16[128,1280]{1,0:T(8,128)(2,1)S(1)}, bf16[128,1280]{1,0:T(8,128)(2,1)S(1)}, u32[]{:S(2)}, u32[]{:S(2)}) collective-permute-start(bf16[128,1280]{1,0:T(8,128)(2,1)S(1)} %bitcast.142), channel_id=1, source_target_pairs={{0,1},{1,0},{2,3},{3,2},{4,5},{5,4},{6,7},{7,6},{8,9},{9,8},{10,11... | collective-permute-start | bytes 983048 | tf_op jit(solution)/shard_map/ppermute | solution.py:42
  285.7 16.5 %collective-permute-start.58 = (bf16[64,1280]{1,0:T(8,128)(2,1)S(1)}, bf16[64,1280]{1,0:T(8,128)(2,1)S(1)}, u32[]{:S(2)}, u32[]{:S(2)}) collective-permute-start(bf16[64,1280]{1,0:T(8,128)(2,1)S(1)} %bitcast.154), channel_id=1, source_target_pairs={{0,1},{1,0},{2,3},{3,2},{4,5},{5,4},{6,7},{7,6},{8,9},{9,8},{10,11... | collective-permute-start | bytes 491528 | tf_op jit(solution)/shard_map/ppermute | solution.py:42
  288.8 12.1 %collective-permute-start.62 = (f32[3,16,1280]{2,1,0:T(8,128)S(1)}, f32[3,16,1280]{2,1,0:T(8,128)S(1)}, u32[]{:S(2)}, u32[]{:S(2)}) collective-permute-start(f32[3,16,1280]{2,1,0:T(8,128)S(1)} %add.314), channel_id=1, source_target_pairs={{0,4},{1,5},{2,6},{3,7},{4,0},{5,1},{6,2},{7,3},{8,12},{9,13},{10,... | collective-permute-start | bytes 737288 | tf_op jit(solution)/shard_map/ppermute | solution.py:42
  (54 other events, 530.7 us)
